TPU v7x, 256 devices: a whole 4x4x8 slice. The times are simulated.
256 devices in a mesh: space: 128 (over x, y, z), rep: 2 (over core).
Axes of the slice: x: 4, y: 4, z: 8, core: 2. Of those that a mesh axis runs over, the one named last changes fastest.
Arguments:
- acts: bfloat16 [3072, 512, 128], P(('space', 'rep')), may hold values from -6 to 6
- preact: bfloat16 [3072, 512, 128], P(('space', 'rep')), may hold values from -8 to 8
- cotangent: bfloat16 [3072, 512, 128], P(('space', 'rep')), may hold values from -6 to 6
- filt: bfloat16 [3456, 128], P('space', 'rep'), may hold values from -0.109375 to 0.109375
- counts: int32 [256], replicated, may hold values from 1 to 12, as said below
- neighbors: int32 [3072, 27], P(('space', 'rep')), may hold values from 0 to 3072, as said below
Outputs:
- input_grad: bfloat16 [3072, 512, 128], P(('space', 'rep'))
- filt_grad: float32 [3456, 128], P('space', 'rep')
Inputs may be any that keep to these rules, and one draw needn't show every extreme that they name: counts[d] is the number of live bricks of device d, which fill its first slots; counts[d] + counts[d xor 1] <= 16, where d xor 1 is the other core of the same chip; in every draw some device holds 12 bricks and its partner 2 * 8 - 12. Brick n = d * 12 + s sits in slab d of the brick grid at one of 5 x 5 places, slot 0 of every device at the middle place; neighbors[n, k] is the index of the live brick at offset off_k (first component along the slabs, so it lies on device d - 1, d or d + 1) from that place, or 3072 where there is none, also for bricks that are not live.
All inputs are finite; a program needn't handle non-finite values.
Results may differ from a plain program's by a relative error of at most 0.0049.
Values may be sent and summed in bfloat16 or wider, within the bound.
A program may use at most 128 MiB of HBM per device.

v0:
```python
import math
import jax
import jax.numpy as jnp
from jax import lax
from jax.sharding import PartitionSpec as P

BRICK = 8
tap_offsets = [
    (step_x, step_y, step_z)
    for step_x in (-1, 0, 1)
    for step_y in (-1, 0, 1)
    for step_z in (-1, 0, 1)
]


def shifted(x, axis, by):
    count = lax.axis_size(axis)
    pairs = [(i, i + by) for i in range(count) if 0 <= i + by < count]
    return lax.ppermute(x, axis, pairs)


def silu_slope(values):
    sigma = jax.nn.sigmoid(values)
    return sigma * (1.0 + values * (1.0 - sigma))


def edge(offset, brick_side):
    if offset < 0:
        return slice(brick_side - 1, brick_side)
    if offset == 0:
        return slice(0, brick_side)
    return slice(0, 1)


def assemble(planes, indices, usable):
    layers = []
    for step_x in range(3):
        strips = []
        for step_y in range(3):
            columns = []
            for step_z in range(3):
                tap = step_x * 9 + step_y * 3 + step_z
                source = planes[step_x]
                brick_side = source.shape[2]
                fetched = jnp.take(source, indices[:, tap], axis=0)
                fetched = fetched[:, :, edge(step_y - 1, brick_side), edge(step_z - 1, brick_side)]
                keeper = usable[:, tap][:, None, None, None, None]
                columns.append(jnp.where(keeper, fetched, jnp.zeros_like(fetched)))
            strips.append(jnp.concatenate(columns, axis=3))
        layers.append(jnp.concatenate(strips, axis=2))
    return jnp.concatenate(layers, axis=1)


def unfold(padded, direction):
    brick_side = padded.shape[0] - 2
    sections = []
    for step_x, step_y, step_z in tap_offsets:
        start_x = 1 + direction * step_x
        start_y = 1 + direction * step_y
        start_z = 1 + direction * step_z
        sections.append(
            padded[
                start_x : start_x + brick_side,
                start_y : start_y + brick_side,
                start_z : start_z + brick_side,
            ]
        )
    return jnp.concatenate(sections, axis=-1).reshape(brick_side**3, -1)


def run_bricks(act_pad, grad_pad, filt_flip, running):

    def per_brick(accum, operands):
        act_block, grad_block = operands
        unrolled_act = unfold(act_block, 1)
        unrolled_grad = unfold(grad_block, -1)
        center = grad_block[1:-1, 1:-1, 1:-1].reshape(-1, grad_block.shape[-1])
        accum = accum + lax.dot_general(
            unrolled_act, center, (((0,), (0,)), ((), ())), preferred_element_type=jnp.float32
        )
        return (accum, jnp.dot(unrolled_grad, filt_flip, preferred_element_type=jnp.float32))

    return lax.scan(per_brick, running, (act_pad, grad_pad))


def on_device(acts, preact, cotangent, filt, counts, neighbors):
    slot_count, voxels, channels = acts.shape
    devices = lax.axis_size(("space", "rep"))
    position = lax.axis_index(("space", "rep"))
    grand_total = slot_count * devices
    live_count = counts[position]
    is_live = jnp.arange(slot_count) < live_count
    grad_pre = jnp.where(
        is_live[:, None, None],
        cotangent.astype(jnp.float32) * silu_slope(preact.astype(jnp.float32)),
        0.0,
    ).astype(jnp.bfloat16)
    gathered_rows = lax.all_gather(filt, "space", axis=0, tiled=True)
    full_filter = lax.all_gather(gathered_rows, "rep", axis=1, tiled=True)
    filt_flip = (
        full_filter.reshape(27, channels, channels)
        .transpose(0, 2, 1)
        .reshape(27 * channels, channels)
    )
    act_five = acts.reshape(slot_count, BRICK, BRICK, BRICK, channels)
    grad_five = grad_pre.reshape(slot_count, BRICK, BRICK, BRICK, channels)
    from_below = shifted((act_five[:, BRICK - 1 :], grad_five[:, BRICK - 1 :]), ("space", "rep"), 1)
    from_above = shifted((act_five[:, :1], grad_five[:, :1]), ("space", "rep"), -1)
    usable = neighbors < grand_total
    slab_step = jnp.arange(27, dtype=jnp.int32) // 9 - 1
    local_slot = jnp.clip(
        neighbors - (position + slab_step[None, :]) * slot_count, 0, slot_count - 1
    )
    act_pad = assemble((from_below[0], act_five, from_above[0]), local_slot, usable)
    grad_pad = assemble((from_below[1], grad_five, from_above[1]), local_slot, usable)
    start = jnp.zeros((27 * channels, channels), jnp.float32)
    filt_sum, grads = run_bricks(act_pad, grad_pad, filt_flip, start)
    brick_grads = grads.astype(jnp.bfloat16)
    input_grad = jnp.where(is_live[:, None, None], brick_grads, jnp.zeros_like(brick_grads))
    inverse_norm = 1.0 / math.sqrt(grand_total * voxels)
    shard_rows = lax.psum_scatter(filt_sum, "space", scatter_dimension=0, tiled=True)
    filt_grad = lax.psum_scatter(shard_rows, "rep", scatter_dimension=1, tiled=True)
    return (input_grad, filt_grad * inverse_norm)


def solution(mesh):
    in_specs = (
        P(("space", "rep"), None, None),
        P(("space", "rep"), None, None),
        P(("space", "rep"), None, None),
        P("space", "rep"),
        P(),
        P(("space", "rep"), None),
    )
    out_specs = (P(("space", "rep"), None, None), P("space", "rep"))
    return jax.shard_map(
        on_device, mesh=mesh, in_specs=in_specs, out_specs=out_specs, check_vma=False
    )
```

profile of v0, /device:TPU:1, one launch (start us, length us, event | category | flops | bytes accessed | tf_op | source)
XLA Modules:
  0.0 1390.8 jit_solution(1618855230662512076)
XLA Ops:
  9.3 3.3 fusion.11
  13.4 5.1 collective-permute-start.3
  21.2 3.6 collective-permute-start.2
  38.6 2.0 gather_fusion.12
  41.3 2.0 gather_fusion.41
  52.7 2.0 gather_fusion.43
  54.7 2.0 gather_fusion.16
  65.9 2.0 gather_fusion.11
  70.8 2.0 gather_fusion.42
  94.1 2.0 gather_fusion.40
  112.0 295.4 %all-gather = bf16[128,27,64]{2,1,0:T(8,128)(2,1)S(1)} all-gather(bf16[1,27,64]{2,1,0:T(8,128)(2,1)S(1)} %bitcast.211), channel_id=1, replica_groups=mesh['space'=128,'rep'=2] {'space'}, dimensions={0}, use_global_device_ids=true | all-gather | bytes 445824 | tf_op jit(solution)/shard_map/all_gather | solution.py:98
  408.1 58.8 %all_gather.7 = bf16[3456,128]{0,1:T(8,128)(2,1)S(1)} all-gather(bf16[3456,64]{0,1:T(8,128)(2,1)S(1)} %copy.9), channel_id=1, replica_groups=mesh['space'=128,'rep'=2] {'rep'}, dimensions={1}, use_global_device_ids=true | all-gather | bytes 1327104 | tf_op jit(solution)/shard_map/all_gather | solution.py:99
  469.3 3.5 select_select_fusion
  472.9 4.8 broadcast_select_fusion.4
  477.7 2.3 fusion.12
  480.0 2.2 broadcast_select_fusion.32
  482.2 2.2 broadcast_select_fusion.28
  487.5 2.2 gather_fusion.21
  489.7 2.2 gather_fusion.23
  493.1 2.2 gather_fusion.19
  496.5 2.2 gather_fusion.25
  499.9 2.2 gather_fusion.18
  503.4 2.2 gather_fusion.20
  506.8 2.2 gather_fusion.24
  510.2 2.2 gather_fusion.26
  514.9 2.2 gather_fusion.5
  517.1 2.2 gather_fusion.3
  520.5 2.2 gather_fusion.7
  523.9 2.2 gather_fusion.1
  527.3 2.2 gather_fusion.6
  530.8 2.2 gather_fusion.8
  534.2 2.2 gather_fusion
  537.6 2.2 gather_fusion.22
  541.2 2.3 gather_fusion.4
  544.8 2.2 gather_fusion.2
  559.2 8.8 maximum_maximum_fusion.1
  568.0 6.8 maximum_maximum_fusion
  574.8 353.8 %while.14 = (s32[]{:T(128)}, f32[3456,128]{1,0:T(8,128)}, bf16[12,512,128]{2,1,0:T(8,128)(2,1)}, bf16[12,10,10,10,128]{4,3,2,1,0:T(8,128)(2,1)}, bf16[12,10,10,1...) while((s32[]{:T(128)}, f32[3456,128]{1,0:T(8,128)}, ...), condition=%wide.region_1.4_spmd.clone.clone, body=%wide.region_0.3_spmd.clone.sunk.clone | while | flops 906854400 | bytes 41230984 | solution.py:83
  598.9 4.2 fusion.52
  628.4 4.2 fusion.52
  657.9 4.2 fusion.52
  687.4 4.2 fusion.52
  716.8 4.2 fusion.52
  746.3 4.2 fusion.52
  775.8 4.2 fusion.52
  805.3 4.2 fusion.52
  834.8 4.2 fusion.52
  864.2 4.2 fusion.52
  893.7 4.2 fusion.52
  923.2 4.2 fusion.52
  928.6 296.9 %fusion = f32[32,128]{1,0:T(8,128)S(1)} fusion(f32[3456,128]{1,0:T(8,128)} %get-tuple-element.38), kind=kCustom, calls=%all-reduce-scatter | all-reduce-scatter fusion | flops 524289 | bytes 1786880
  1234.1 7.0 collective-permute-start.15
  1243.7 5.8 collective-permute-start.18
  1249.5 22.4 %collective-permute-start.19 = (f32[32,128]{1,0:T(8,128)S(1)}, f32[32,128]{1,0:T(8,128)S(1)}, u32[]{:S(2)}, u32[]{:S(2)}) collective-permute-start(f32[32,128]{1,0:T(8,128)S(1)} %fusion), channel_id=1, source_target_pairs={{0,32},{2,34},{4,36},{6,38},{8,40},{10,42},{12,44},{14,46},{16,48}... | collective-permute-start | bytes 49160
  1272.0 2.5 collective-permute-start.20
  1274.5 7.8 collective-permute-start.21
  1282.4 4.9 collective-permute-start.22
  1287.3 2.2 collective-permute-start.4
  1291.5 4.6 collective-permute-start.6
  1296.1 4.3 collective-permute-start.7
  1300.4 4.0 collective-permute-start.8
  1304.4 2.2 collective-permute-start.9
  1308.0 2.6 concatenate.112
  1312.7 69.8 %reduce-scatter.6.cloned.1.call-done = f32[64,27]{1,0:T(8,128)} async-done(((f32[128,27]{1,0:T(8,128)}), f32[64,27]{1,0:T(8,128)}) %reduce-scatter.6.cloned.1.call-update) | async-done | bytes 6928
  (990 shorter events, 435.4 us)
Async XLA Ops:
  7.2 11.3 copy-start
  7.2 19.6 %copy-start.14 = (s32[12,27]{1,0:T(8,128)S(1)}, s32[12,27]{1,0:T(8,128)}, u32[]{:S(2)}) copy-start(s32[12,27]{1,0:T(8,128)} %param.17) | copy-start | bytes 3892
  7.2 1375.3 %reduce-scatter.6.cloned.1.call-start = ((), (), s32[]{:S(2)}) async-start(), calls=%async_computation.1 | async-start | bytes 98304
  7.2 22.8 %copy-start.15 = (s32[12,27]{1,0:T(8,128)S(1)}, s32[12,27]{1,0:T(8,128)}, u32[]{:S(2)}) copy-start(s32[12,27]{1,0:T(8,128)} %param.17) | copy-start | bytes 3892
  13.4 471.6 %collective-permute-start.3 = (bf16[12,1,8,8,128]{4,3,2,1,0:T(8,128)(2,1)}, bf16[12,1,8,8,128]{4,3,2,1,0:T(8,128)(2,1)S(1)}, u32[]{:S(2)}, u32[]{:S(2)}) collective-permute-start(bf16[12,1,8,8,128]{4,3,2,1,0:T(8,128)(2,1)} %get-tuple-element.129), channel_id=1, source_target_pairs={{1,0},{2,1},{3,2},{4,3},{5,4},{6,5},{7,6},{8,7},{9,8},{10,9},{11,1... | collective-permute-start | bytes 589832 | tf_op jit(solution)/shard_map/ppermute | solution.py:19
  19.3 468.2 %collective-permute-start.1 = (bf16[12,1,8,8,128]{4,3,2,1,0:T(8,128)(2,1)}, bf16[12,1,8,8,128]{4,3,2,1,0:T(8,128)(2,1)}, u32[]{:S(2)}, u32[]{:S(2)}) collective-permute-start(bf16[12,1,8,8,128]{4,3,2,1,0:T(8,128)(2,1)} %get-tuple-element.131), channel_id=1, source_target_pairs={{1,0},{2,1},{3,2},{4,3},{5,4},{6,5},{7,6},{8,7},{9,8},{10,9},{11,1... | collective-permute-start | bytes 589832 | tf_op jit(solution)/shard_map/ppermute | solution.py:19
  21.2 491.2 %collective-permute-start.2 = (bf16[12,1,8,8,128]{4,3,2,1,0:T(8,128)(2,1)}, bf16[12,1,8,8,128]{4,3,2,1,0:T(8,128)(2,1)S(1)}, u32[]{:S(2)}, u32[]{:S(2)}) collective-permute-start(bf16[12,1,8,8,128]{4,3,2,1,0:T(8,128)(2,1)} %get-tuple-element.128), channel_id=1, source_target_pairs={{0,1},{1,2},{2,3},{3,4},{4,5},{5,6},{6,7},{7,8},{8,9},{9,10},{10,1... | collective-permute-start | bytes 589832 | tf_op jit(solution)/shard_map/ppermute | solution.py:19
  24.8 490.1 %collective-permute-start = (bf16[12,1,8,8,128]{4,3,2,1,0:T(8,128)(2,1)}, bf16[12,1,8,8,128]{4,3,2,1,0:T(8,128)(2,1)}, u32[]{:S(2)}, u32[]{:S(2)}) collective-permute-start(bf16[12,1,8,8,128]{4,3,2,1,0:T(8,128)(2,1)} %get-tuple-element.130), channel_id=1, source_target_pairs={{0,1},{1,2},{2,3},{3,4},{4,5},{5,6},{6,7},{7,8},{8,9},{9,10},{10,1... | collective-permute-start | bytes 589832 | tf_op jit(solution)/shard_map/ppermute | solution.py:19
  27.8 8.8 copy-start.43
  82.4 29.6 %copy-start.29 = (s32[12]{0:T(128)}, s32[12]{0:T(128)S(1)}, u32[]{:S(2)}) copy-start(s32[12]{0:T(128)S(1)} %get-tuple-element.86) | copy-start | bytes 148
  82.4 29.6 %copy-start.16 = (bf16[27,64]{1,0:T(8,128)(2,1)S(1)}, bf16[27,64]{1,0:T(8,128)(2,1)}, u32[]{:S(2)}) copy-start(bf16[27,64]{1,0:T(8,128)(2,1)} %param.15) | copy-start | bytes 10372
  407.7 61.5 %copy-start.35 = (pred[12]{0:T(512)(128)(4,1)S(1)}, pred[12]{0:T(512)(128)(4,1)}, u32[]{:S(2)}) copy-start(pred[12]{0:T(512)(128)(4,1)} %get-tuple-element.101) | copy-start | bytes 40
  407.7 61.5 %copy-start.36 = (pred[12]{0:T(512)(128)(4,1)S(1)}, pred[12]{0:T(512)(128)(4,1)}, u32[]{:S(2)}) copy-start(pred[12]{0:T(512)(128)(4,1)} %get-tuple-element.202) | copy-start | bytes 40
  472.8 9.4 copy-start.23
  472.8 9.4 copy-start.24
  472.8 9.4 copy-start.41
  472.8 9.4 copy-start.42
  472.8 11.6 copy-start.30
  522.7 28.5 %copy-start.21 = (pred[12]{0:T(512)(128)(4,1)S(1)}, pred[12]{0:T(512)(128)(4,1)}, u32[]{:S(2)}) copy-start(pred[12]{0:T(512)(128)(4,1)} %get-tuple-element.91) | copy-start | bytes 40
  522.7 28.5 %copy-start.22 = (pred[12]{0:T(512)(128)(4,1)S(1)}, pred[12]{0:T(512)(128)(4,1)}, u32[]{:S(2)}) copy-start(pred[12]{0:T(512)(128)(4,1)} %get-tuple-element.93) | copy-start | bytes 40
  523.9 28.8 %copy-start.19 = (pred[12]{0:T(512)(128)(4,1)S(1)}, pred[12]{0:T(512)(128)(4,1)}, u32[]{:S(2)}) copy-start(pred[12]{0:T(512)(128)(4,1)} %get-tuple-element.89) | copy-start | bytes 40
  523.9 28.9 %copy-start.20 = (pred[12]{0:T(512)(128)(4,1)S(1)}, pred[12]{0:T(512)(128)(4,1)}, u32[]{:S(2)}) copy-start(pred[12]{0:T(512)(128)(4,1)} %get-tuple-element.95) | copy-start | bytes 40
  526.1 28.6 %copy-start.17 = (pred[12]{0:T(512)(128)(4,1)S(1)}, pred[12]{0:T(512)(128)(4,1)}, u32[]{:S(2)}) copy-start(pred[12]{0:T(512)(128)(4,1)} %get-tuple-element.88) | copy-start | bytes 40
  526.1 28.6 %copy-start.18 = (pred[12]{0:T(512)(128)(4,1)S(1)}, pred[12]{0:T(512)(128)(4,1)}, u32[]{:S(2)}) copy-start(pred[12]{0:T(512)(128)(4,1)} %get-tuple-element.90) | copy-start | bytes 40
  537.6 21.4 %copy-start.5 = (bf16[12,8,8,1,128]{4,3,2,1,0:T(2,128)(2,1)S(1)}, bf16[12,8,8,1,128]{4,3,2,1,0:T(2,128)(2,1)}, u32[]{:S(2)}) copy-start(bf16[12,8,8,1,128]{4,3,2,1,0:T(2,128)(2,1)} %get-tuple-element.160) | copy-start | bytes 589828
  544.8 14.3 %copy-start.9 = (bf16[12,8,1,8,128]{4,3,2,1,0:T(8,128)(2,1)S(1)}, bf16[12,8,1,8,128]{4,3,2,1,0:T(8,128)(2,1)}, u32[]{:S(2)}) copy-start(bf16[12,8,1,8,128]{4,3,2,1,0:T(8,128)(2,1)} %get-tuple-element.164) | copy-start | bytes 589828
  547.0 12.1 copy-start.1
  559.1 8.8 copy-start.4
  559.1 8.8 copy-start.7
  574.8 731.8 %copy-start.46 = (u32[256]{0:T(256)S(1)}, u32[256]{0:T(256)}, u32[]{:S(2)}) copy-start(u32[256]{0:T(256)} %constant.87) | copy-start | bytes 3076
  574.8 736.5 %copy-start.32 = (pred[12]{0:T(512)(128)(4,1)S(1)}, pred[12]{0:T(512)(128)(4,1)}, u32[]{:S(2)}) copy-start(pred[12]{0:T(512)(128)(4,1)} %copy-done.31) | copy-start | bytes 40
  579.6 19.3 %copy-start.2 = (f32[3456,128]{1,0:T(8,128)S(1)}, f32[3456,128]{1,0:T(8,128)}, u32[]{:S(2)}) copy-start(f32[3456,128]{1,0:T(8,128)} %get-tuple-element.277) | copy-start | bytes 5308420 | tf_op jit(solution)/shard_map/while
  609.1 19.3 %copy-start.2 = (f32[3456,128]{1,0:T(8,128)S(1)}, f32[3456,128]{1,0:T(8,128)}, u32[]{:S(2)}) copy-start(f32[3456,128]{1,0:T(8,128)} %get-tuple-element.277) | copy-start | bytes 5308420 | tf_op jit(solution)/shard_map/while
  638.6 19.3 %copy-start.2 = (f32[3456,128]{1,0:T(8,128)S(1)}, f32[3456,128]{1,0:T(8,128)}, u32[]{:S(2)}) copy-start(f32[3456,128]{1,0:T(8,128)} %get-tuple-element.277) | copy-start | bytes 5308420 | tf_op jit(solution)/shard_map/while
  668.0 19.3 %copy-start.2 = (f32[3456,128]{1,0:T(8,128)S(1)}, f32[3456,128]{1,0:T(8,128)}, u32[]{:S(2)}) copy-start(f32[3456,128]{1,0:T(8,128)} %get-tuple-element.277) | copy-start | bytes 5308420 | tf_op jit(solution)/shard_map/while
  697.5 19.3 %copy-start.2 = (f32[3456,128]{1,0:T(8,128)S(1)}, f32[3456,128]{1,0:T(8,128)}, u32[]{:S(2)}) copy-start(f32[3456,128]{1,0:T(8,128)} %get-tuple-element.277) | copy-start | bytes 5308420 | tf_op jit(solution)/shard_map/while
  727.0 19.3 %copy-start.2 = (f32[3456,128]{1,0:T(8,128)S(1)}, f32[3456,128]{1,0:T(8,128)}, u32[]{:S(2)}) copy-start(f32[3456,128]{1,0:T(8,128)} %get-tuple-element.277) | copy-start | bytes 5308420 | tf_op jit(solution)/shard_map/while
  756.5 19.3 %copy-start.2 = (f32[3456,128]{1,0:T(8,128)S(1)}, f32[3456,128]{1,0:T(8,128)}, u32[]{:S(2)}) copy-start(f32[3456,128]{1,0:T(8,128)} %get-tuple-element.277) | copy-start | bytes 5308420 | tf_op jit(solution)/shard_map/while
  786.0 19.3 %copy-start.2 = (f32[3456,128]{1,0:T(8,128)S(1)}, f32[3456,128]{1,0:T(8,128)}, u32[]{:S(2)}) copy-start(f32[3456,128]{1,0:T(8,128)} %get-tuple-element.277) | copy-start | bytes 5308420 | tf_op jit(solution)/shard_map/while
  815.4 19.3 %copy-start.2 = (f32[3456,128]{1,0:T(8,128)S(1)}, f32[3456,128]{1,0:T(8,128)}, u32[]{:S(2)}) copy-start(f32[3456,128]{1,0:T(8,128)} %get-tuple-element.277) | copy-start | bytes 5308420 | tf_op jit(solution)/shard_map/while
  844.9 19.3 %copy-start.2 = (f32[3456,128]{1,0:T(8,128)S(1)}, f32[3456,128]{1,0:T(8,128)}, u32[]{:S(2)}) copy-start(f32[3456,128]{1,0:T(8,128)} %get-tuple-element.277) | copy-start | bytes 5308420 | tf_op jit(solution)/shard_map/while
  874.4 19.3 %copy-start.2 = (f32[3456,128]{1,0:T(8,128)S(1)}, f32[3456,128]{1,0:T(8,128)}, u32[]{:S(2)}) copy-start(f32[3456,128]{1,0:T(8,128)} %get-tuple-element.277) | copy-start | bytes 5308420 | tf_op jit(solution)/shard_map/while
  903.9 19.3 %copy-start.2 = (f32[3456,128]{1,0:T(8,128)S(1)}, f32[3456,128]{1,0:T(8,128)}, u32[]{:S(2)}) copy-start(f32[3456,128]{1,0:T(8,128)} %get-tuple-element.277) | copy-start | bytes 5308420 | tf_op jit(solution)/shard_map/while
  928.6 382.7 %copy-start.6 = (bf16[12,512,128]{2,1,0:T(8,128)(2,1)S(1)}, bf16[12,512,128]{2,1,0:T(8,128)(2,1)}, u32[]{:S(2)}) copy-start(bf16[12,512,128]{2,1,0:T(8,128)(2,1)} %get-tuple-element.37) | copy-start | bytes 4718596
  1225.5 8.6 collective-permute-start.10
  1226.8 14.3 %collective-permute-start.11 = (f32[32,128]{1,0:T(8,128)S(1)}, f32[32,128]{1,0:T(8,128)S(1)}, u32[]{:S(2)}, u32[]{:S(2)}) collective-permute-start(f32[32,128]{1,0:T(8,128)S(1)} %fusion), channel_id=1, source_target_pairs={{0,16},{2,18},{4,20},{6,22},{8,24},{10,26},{12,28},{14,30},{16,32}... | collective-permute-start | bytes 49160
  1228.1 14.3 %collective-permute-start.12 = (f32[32,128]{1,0:T(8,128)S(1)}, f32[32,128]{1,0:T(8,128)S(1)}, u32[]{:S(2)}, u32[]{:S(2)}) collective-permute-start(f32[32,128]{1,0:T(8,128)S(1)} %fusion), channel_id=1, source_target_pairs={{0,18},{2,20},{4,22},{6,24},{8,26},{10,28},{12,30},{14,32},{16,34}... | collective-permute-start | bytes 49160
  1229.4 14.3 %collective-permute-start.13 = (f32[32,128]{1,0:T(8,128)S(1)}, f32[32,128]{1,0:T(8,128)S(1)}, u32[]{:S(2)}, u32[]{:S(2)}) collective-permute-start(f32[32,128]{1,0:T(8,128)S(1)} %fusion), channel_id=1, source_target_pairs={{0,20},{2,22},{4,24},{6,26},{8,28},{10,30},{12,32},{14,34},{16,36}... | collective-permute-start | bytes 49160
  1230.7 2.1 collective-permute-start.23
  1232.8 16.7 %collective-permute-start.14 = (f32[32,128]{1,0:T(8,128)S(1)}, f32[32,128]{1,0:T(8,128)S(1)}, u32[]{:S(2)}, u32[]{:S(2)}) collective-permute-start(f32[32,128]{1,0:T(8,128)S(1)} %fusion), channel_id=1, source_target_pairs={{0,22},{2,24},{4,26},{6,28},{8,30},{10,32},{12,34},{14,36},{16,38}... | collective-permute-start | bytes 49160
  1234.1 37.8 %collective-permute-start.15 = (f32[32,128]{1,0:T(8,128)S(1)}, f32[32,128]{1,0:T(8,128)S(1)}, u32[]{:S(2)}, u32[]{:S(2)}) collective-permute-start(f32[32,128]{1,0:T(8,128)S(1)} %fusion), channel_id=1, source_target_pairs={{0,24},{2,26},{4,28},{6,30},{8,32},{10,34},{12,36},{14,38},{16,40}... | collective-permute-start | bytes 49160
  1241.1 33.4 %collective-permute-start.16 = (f32[32,128]{1,0:T(8,128)S(1)}, f32[32,128]{1,0:T(8,128)S(1)}, u32[]{:S(2)}, u32[]{:S(2)}) collective-permute-start(f32[32,128]{1,0:T(8,128)S(1)} %fusion), channel_id=1, source_target_pairs={{0,26},{2,28},{4,30},{6,32},{8,34},{10,36},{12,38},{14,40},{16,42}... | collective-permute-start | bytes 49160
  1242.4 40.0 %collective-permute-start.17 = (f32[32,128]{1,0:T(8,128)S(1)}, f32[32,128]{1,0:T(8,128)S(1)}, u32[]{:S(2)}, u32[]{:S(2)}) collective-permute-start(f32[32,128]{1,0:T(8,128)S(1)} %fusion), channel_id=1, source_target_pairs={{0,28},{2,30},{4,32},{6,34},{8,36},{10,38},{12,40},{14,42},{16,44}... | collective-permute-start | bytes 49160
  1243.7 43.6 %collective-permute-start.18 = (f32[32,128]{1,0:T(8,128)S(1)}, f32[32,128]{1,0:T(8,128)S(1)}, u32[]{:S(2)}, u32[]{:S(2)}) collective-permute-start(f32[32,128]{1,0:T(8,128)S(1)} %fusion), channel_id=1, source_target_pairs={{0,30},{2,32},{4,34},{6,36},{8,38},{10,40},{12,42},{14,44},{16,46}... | collective-permute-start | bytes 49160
  1249.5 40.0 %collective-permute-start.19 = (f32[32,128]{1,0:T(8,128)S(1)}, f32[32,128]{1,0:T(8,128)S(1)}, u32[]{:S(2)}, u32[]{:S(2)}) collective-permute-start(f32[32,128]{1,0:T(8,128)S(1)} %fusion), channel_id=1, source_target_pairs={{0,32},{2,34},{4,36},{6,38},{8,40},{10,42},{12,44},{14,46},{16,48}... | collective-permute-start | bytes 49160
  1272.0 19.5 %collective-permute-start.20 = (f32[32,128]{1,0:T(8,128)S(1)}, f32[32,128]{1,0:T(8,128)S(1)}, u32[]{:S(2)}, u32[]{:S(2)}) collective-permute-start(f32[32,128]{1,0:T(8,128)S(1)} %fusion), channel_id=1, source_target_pairs={{0,34},{2,36},{4,38},{6,40},{8,42},{10,44},{12,46},{14,48},{16,50}... | collective-permute-start | bytes 49160
  1274.5 21.5 %collective-permute-start.21 = (f32[32,128]{1,0:T(8,128)S(1)}, f32[32,128]{1,0:T(8,128)S(1)}, u32[]{:S(2)}, u32[]{:S(2)}) collective-permute-start(f32[32,128]{1,0:T(8,128)S(1)} %fusion), channel_id=1, source_target_pairs={{0,36},{2,38},{4,40},{6,42},{8,44},{10,46},{12,48},{14,50},{16,52}... | collective-permute-start | bytes 49160
  1282.4 18.0 %collective-permute-start.22 = (f32[32,128]{1,0:T(8,128)S(1)}, f32[32,128]{1,0:T(8,128)S(1)}, u32[]{:S(2)}, u32[]{:S(2)}) collective-permute-start(f32[32,128]{1,0:T(8,128)S(1)} %fusion), channel_id=1, source_target_pairs={{0,38},{2,40},{4,42},{6,44},{8,46},{10,48},{12,50},{14,52},{16,54}... | collective-permute-start | bytes 49160
  1287.3 17.1 %collective-permute-start.4 = (f32[32,128]{1,0:T(8,128)S(1)}, f32[32,128]{1,0:T(8,128)S(1)}, u32[]{:S(2)}, u32[]{:S(2)}) collective-permute-start(f32[32,128]{1,0:T(8,128)S(1)} %fusion), channel_id=1, source_target_pairs={{0,2},{2,4},{4,6},{6,8},{8,10},{10,12},{12,14},{14,16},{16,18},{18... | collective-permute-start | bytes 49160
  1289.5 18.4 %collective-permute-start.5 = (f32[32,128]{1,0:T(8,128)S(1)}, f32[32,128]{1,0:T(8,128)S(1)}, u32[]{:S(2)}, u32[]{:S(2)}) collective-permute-start(f32[32,128]{1,0:T(8,128)S(1)} %fusion), channel_id=1, source_target_pairs={{0,4},{2,6},{4,8},{6,10},{8,12},{10,14},{12,16},{14,18},{16,20},{1... | collective-permute-start | bytes 49160
  1291.5 16.4 %collective-permute-start.6 = (f32[32,128]{1,0:T(8,128)S(1)}, f32[32,128]{1,0:T(8,128)S(1)}, u32[]{:S(2)}, u32[]{:S(2)}) collective-permute-start(f32[32,128]{1,0:T(8,128)S(1)} %fusion), channel_id=1, source_target_pairs={{0,6},{2,8},{4,10},{6,12},{8,14},{10,16},{12,18},{14,20},{16,22},{... | collective-permute-start | bytes 49160
  1296.1 11.9 collective-permute-start.7
  1300.4 7.5 collective-permute-start.8
  1304.4 3.5 collective-permute-start.9
  (30 other events, 139.6 us)
Sparse Core Ops, SparseCore 0:
  1311.4 71.0 reduce-scatter.5
where the time goes:
time: 1390 us
  blocking collectives  651 us (47%)
  local copies, waits for them, and re-layouts  392 us (28%)
  other arithmetic  94.9 us (7%)
  starting transfers between devices  92.6 us (7%)
  matrix products  71.2 us (5%)
  waiting for transfers between devices  70.8 us (5%)
  between operations  15.7 us (1%)
    unnamed x1, blocking collectives  297 us
    all_gather x1, blocking collectives, on_device(): gathered_rows = lax.all_gather(filt, 'space', axis=0, tiled=True)  295 us
    while x672, local copies, waits for them, and re-layouts  256 us
    gather x54, local copies, waits for them, and re-layouts, assemble(): fetched = jnp.take(source, indices[:, tap], axis=0)  97.3 us
    unnamed x21, starting transfers between devices  80 us
    unnamed x22, waiting for transfers between devices  70.8 us
    all_gather x1, blocking collectives, on_device(): full_filter = lax.all_gather(gathered_rows, 'rep', axis=1, tiled=True)  58.8 us
    dot_general x12, matrix products, per_brick(): lax.dot_general(unrolled_act, center, (((0,), (0,)), ((), ())), preferred...  50.3 us
  transfers between devices with their start and end apart: 25, of which 2 were waited for; matrix products, arithmetic and copies ran while one was open for 10% of the time, Pallas kernels for 0%

commit v1 on v0

--- a/solution.py
+++ b/solution.py
@@ -96,7 +96,10 @@
         0.0,
     ).astype(jnp.bfloat16)
     gathered_rows = lax.all_gather(filt, "space", axis=0, tiled=True)
-    full_filter = lax.all_gather(gathered_rows, "rep", axis=1, tiled=True)
+    size = lax.axis_size("rep")
+    parts = jnp.stack([gathered_rows for _ in range(size)])
+    parts = lax.all_to_all(parts, "rep", split_axis=0, concat_axis=0)
+    full_filter = jnp.concatenate(parts, axis=1)
     filt_flip = (
         full_filter.reshape(27, channels, channels)
         .transpose(0, 2, 1)

time: 1390 us -> 1420 us (1.022)
  starting transfers between devices: 92.6 us -> 154 us
  blocking collectives: 651 us -> 611 us
    all_to_all x0 -> x1, starting transfers between devices: none -> 62 us  [on_device(): parts = lax.all_to_all(parts, 'rep', split_axis=0, concat_axis=0)]
    all_gather x1 -> x0, blocking collectives: 58.8 us -> none  [on_device(): full_filter = lax.all_gather(gathered_rows, 'rep', axis=1, tiled=True)]
    all_gather x1, blocking collectives: 295 us -> 314 us  [on_device(): gathered_rows = lax.all_gather(filt, 'space', axis=0, tiled=True)]
  transfers between devices with their start and end apart: 25 -> 26, of which waited for: 2 -> 2; matrix products, arithmetic and copies ran while one was open for 10% -> 10% of each run, Pallas kernels for 0% -> 0%
where the time goes in v1:
time: 1420 us
  blocking collectives  611 us (43%)
  local copies, waits for them, and re-layouts  396 us (28%)
  starting transfers between devices  154 us (11%)
  other arithmetic  98.9 us (7%)
  matrix products  71.2 us (5%)
  waiting for transfers between devices  70.4 us (5%)
  between operations  15.7 us (1%)
    all_gather x1, blocking collectives, on_device(): gathered_rows = lax.all_gather(filt, 'space', axis=0, tiled=True)  314 us
    unnamed x1, blocking collectives  297 us
    while x672, local copies, waits for them, and re-layouts  256 us
    gather x54, local copies, waits for them, and re-layouts, assemble(): fetched = jnp.take(source, indices[:, tap], axis=0)  97.1 us
    unnamed x21, starting transfers between devices  79.9 us
    unnamed x22, waiting for transfers between devices  70.4 us
    all_to_all x1, starting transfers between devices, on_device(): parts = lax.all_to_all(parts, 'rep', split_axis=0, concat_axis=0)  62 us
    dot_general x12, matrix products, per_brick(): lax.dot_general(unrolled_act, center, (((0,), (0,)), ((), ())), preferred...  50.3 us
  transfers between devices with their start and end apart: 26, of which 2 were waited for; matrix products, arithmetic and copies ran while one was open for 10% of the time, Pallas kernels for 0%

profile of v1, /device:TPU:1, one launch (start us, length us, event | category | flops | bytes accessed | tf_op | source)
XLA Modules:
  0.0 1419.9 jit_solution(5518230740062316495)
XLA Ops:
  9.2 3.3 fusion.11
  13.3 5.1 collective-permute-start.3
  21.1 3.6 collective-permute-start.2
  26.7 314.2 %all-gather = bf16[128,27,64]{2,1,0:T(8,128)(2,1)} all-gather(bf16[1,27,64]{2,1,0:T(8,128)(2,1)S(1)} %bitcast.212), channel_id=1, replica_groups=mesh['space'=128,'rep'=2] {'space'}, dimensions={0}, use_global_device_ids=true | all-gather | bytes 445824 | tf_op jit(solution)/shard_map/all_gather | solution.py:98
  340.9 2.2 stack.7
  343.2 3.1 pad_maximum_fusion
  346.2 2.5 copy.11
  348.8 62.0 %all-to-all-start = ((bf16[2,3456,64]{1,2,0:T(8,128)(2,1)}), bf16[2,3456,64]{1,2,0:T(8,128)(2,1)}, u32[]{:S(2)}, u32[]{:S(2)}) async-start(bf16[2,3456,64]{1,2,0:T(8,128)(2,1)} %copy.11), calls=%async_computation | async-start | bytes 1769472 | tf_op jit(solution)/shard_map/all_to_all | solution.py:101
  423.3 2.0 gather_fusion.12
  425.9 2.0 gather_fusion.41
  451.0 2.0 gather_fusion.11
  479.8 2.0 gather_fusion.40
  499.3 3.5 select_select_fusion
  502.9 4.8 broadcast_select_fusion.4
  507.7 2.3 fusion.12
  510.0 2.2 broadcast_select_fusion.32
  512.3 2.2 broadcast_select_fusion.28
  517.5 2.2 gather_fusion.21
  519.7 2.2 gather_fusion.23
  523.1 2.2 gather_fusion.19
  526.6 2.2 gather_fusion.25
  530.0 2.2 gather_fusion.18
  533.4 2.2 gather_fusion.20
  536.8 2.2 gather_fusion.24
  540.3 2.2 gather_fusion.26
  544.9 2.2 gather_fusion.5
  547.1 2.2 gather_fusion.3
  550.6 2.2 gather_fusion.7
  554.0 2.2 gather_fusion.1
  557.4 2.2 gather_fusion.6
  560.9 2.2 gather_fusion.8
  564.3 2.2 gather_fusion
  567.7 2.2 gather_fusion.22
  571.2 2.2 gather_fusion.4
  574.6 2.2 gather_fusion.2
  588.9 8.8 maximum_maximum_fusion.1
  597.7 6.8 maximum_maximum_fusion
  604.5 353.8 %while.14 = (s32[]{:T(128)}, f32[3456,128]{1,0:T(8,128)}, bf16[12,512,128]{2,1,0:T(8,128)(2,1)}, bf16[12,10,10,10,128]{4,3,2,1,0:T(8,128)(2,1)}, bf16[12,10,10,1...) while((s32[]{:T(128)}, f32[3456,128]{1,0:T(8,128)}, ...), condition=%wide.region_1.4_spmd.clone.clone, body=%wide.region_0.3_spmd.clone.sunk.clone | while | flops 906854400 | bytes 41230984 | solution.py:83
  628.6 4.2 fusion.52
  658.1 4.2 fusion.52
  687.6 4.2 fusion.52
  717.1 4.2 fusion.52
  746.5 4.2 fusion.52
  776.0 4.2 fusion.52
  805.5 4.2 fusion.52
  835.0 4.2 fusion.52
  864.5 4.2 fusion.52
  893.9 4.2 fusion.52
  923.4 4.2 fusion.52
  952.9 4.2 fusion.52
  958.3 296.8 %fusion = f32[32,128]{1,0:T(8,128)S(1)} fusion(f32[3456,128]{1,0:T(8,128)} %get-tuple-element.38), kind=kCustom, calls=%all-reduce-scatter | all-reduce-scatter fusion | flops 524289 | bytes 1786880
  1263.7 6.9 collective-permute-start.15
  1273.2 6.1 collective-permute-start.18
  1279.3 22.1 %collective-permute-start.19 = (f32[32,128]{1,0:T(8,128)S(1)}, f32[32,128]{1,0:T(8,128)S(1)}, u32[]{:S(2)}, u32[]{:S(2)}) collective-permute-start(f32[32,128]{1,0:T(8,128)S(1)} %fusion), channel_id=1, source_target_pairs={{0,32},{2,34},{4,36},{6,38},{8,40},{10,42},{12,44},{14,46},{16,48}... | collective-permute-start | bytes 49160
  1301.4 2.5 collective-permute-start.20
  1304.0 7.8 collective-permute-start.21
  1311.9 4.9 collective-permute-start.22
  1316.8 2.2 collective-permute-start.4
  1321.0 4.6 collective-permute-start.6
  1325.5 4.3 collective-permute-start.7
  1329.9 4.0 collective-permute-start.8
  1333.9 2.2 collective-permute-start.9
  1337.4 2.6 concatenate.112
  1342.1 69.4 %reduce-scatter.6.cloned.1.call-done = f32[64,27]{1,0:T(8,128)} async-done(((f32[128,27]{1,0:T(8,128)}), f32[64,27]{1,0:T(8,128)}) %reduce-scatter.6.cloned.1.call-update) | async-done | bytes 6928
  (982 shorter events, 441.3 us)
Async XLA Ops:
  7.2 11.2 copy-start
  7.2 19.5 %copy-start.15 = (bf16[27,64]{1,0:T(8,128)(2,1)S(1)}, bf16[27,64]{1,0:T(8,128)(2,1)}, u32[]{:S(2)}) copy-start(bf16[27,64]{1,0:T(8,128)(2,1)} %param.15) | copy-start | bytes 10372
  13.3 501.7 %collective-permute-start.3 = (bf16[12,1,8,8,128]{4,3,2,1,0:T(8,128)(2,1)}, bf16[12,1,8,8,128]{4,3,2,1,0:T(8,128)(2,1)S(1)}, u32[]{:S(2)}, u32[]{:S(2)}) collective-permute-start(bf16[12,1,8,8,128]{4,3,2,1,0:T(8,128)(2,1)} %get-tuple-element.129), channel_id=1, source_target_pairs={{1,0},{2,1},{3,2},{4,3},{5,4},{6,5},{7,6},{8,7},{9,8},{10,9},{11,1... | collective-permute-start | bytes 589832 | tf_op jit(solution)/shard_map/ppermute | solution.py:19
  19.2 498.3 %collective-permute-start.1 = (bf16[12,1,8,8,128]{4,3,2,1,0:T(8,128)(2,1)}, bf16[12,1,8,8,128]{4,3,2,1,0:T(8,128)(2,1)}, u32[]{:S(2)}, u32[]{:S(2)}) collective-permute-start(bf16[12,1,8,8,128]{4,3,2,1,0:T(8,128)(2,1)} %get-tuple-element.131), channel_id=1, source_target_pairs={{1,0},{2,1},{3,2},{4,3},{5,4},{6,5},{7,6},{8,7},{9,8},{10,9},{11,1... | collective-permute-start | bytes 589832 | tf_op jit(solution)/shard_map/ppermute | solution.py:19
  21.1 521.3 %collective-permute-start.2 = (bf16[12,1,8,8,128]{4,3,2,1,0:T(8,128)(2,1)}, bf16[12,1,8,8,128]{4,3,2,1,0:T(8,128)(2,1)S(1)}, u32[]{:S(2)}, u32[]{:S(2)}) collective-permute-start(bf16[12,1,8,8,128]{4,3,2,1,0:T(8,128)(2,1)} %get-tuple-element.128), channel_id=1, source_target_pairs={{0,1},{1,2},{2,3},{3,4},{4,5},{5,6},{6,7},{7,8},{8,9},{9,10},{10,1... | collective-permute-start | bytes 589832 | tf_op jit(solution)/shard_map/ppermute | solution.py:19
  24.8 520.2 %collective-permute-start = (bf16[12,1,8,8,128]{4,3,2,1,0:T(8,128)(2,1)}, bf16[12,1,8,8,128]{4,3,2,1,0:T(8,128)(2,1)}, u32[]{:S(2)}, u32[]{:S(2)}) collective-permute-start(bf16[12,1,8,8,128]{4,3,2,1,0:T(8,128)(2,1)} %get-tuple-element.130), channel_id=1, source_target_pairs={{0,1},{1,2},{2,3},{3,4},{4,5},{5,6},{6,7},{7,8},{8,9},{9,10},{10,1... | collective-permute-start | bytes 589832 | tf_op jit(solution)/shard_map/ppermute | solution.py:19
  343.2 67.6 %copy-start.14 = (s32[12,27]{1,0:T(8,128)S(1)}, s32[12,27]{1,0:T(8,128)}, u32[]{:S(2)}) copy-start(s32[12,27]{1,0:T(8,128)} %param.17) | copy-start | bytes 3892
  348.8 148.3 %all-to-all-start = ((bf16[2,3456,64]{1,2,0:T(8,128)(2,1)}), bf16[2,3456,64]{1,2,0:T(8,128)(2,1)}, u32[]{:S(2)}, u32[]{:S(2)}) async-start(bf16[2,3456,64]{1,2,0:T(8,128)(2,1)} %copy.11), calls=%async_computation | async-start | bytes 1769472 | tf_op jit(solution)/shard_map/all_to_all | solution.py:101
  410.8 1000.8 %reduce-scatter.6.cloned.1.call-start = ((), (), s32[]{:S(2)}) async-start(), calls=%async_computation.2 | async-start | bytes 98304
  411.9 9.4 copy-start.38
  472.0 24.4 %copy-start.24 = (s32[12]{0:T(128)S(1)}, s32[12]{0:T(128)}, u32[]{:S(2)}) copy-start(s32[12]{0:T(128)} %get-tuple-element.86) | copy-start | bytes 148
  481.8 17.5 %copy-start.30 = (pred[12]{0:T(512)(128)(4,1)S(1)}, pred[12]{0:T(512)(128)(4,1)}, u32[]{:S(2)}) copy-start(pred[12]{0:T(512)(128)(4,1)} %get-tuple-element.101) | copy-start | bytes 40
  481.8 17.5 %copy-start.31 = (pred[12]{0:T(512)(128)(4,1)S(1)}, pred[12]{0:T(512)(128)(4,1)}, u32[]{:S(2)}) copy-start(pred[12]{0:T(512)(128)(4,1)} %get-tuple-element.202) | copy-start | bytes 40
  502.8 9.4 copy-start.18
  502.9 9.4 copy-start.19
  502.9 9.4 copy-start.36
  502.9 9.4 copy-start.37
  502.9 11.6 copy-start.25
  556.2 26.3 %copy-start.17 = (pred[12]{0:T(512)(128)(4,1)S(1)}, pred[12]{0:T(512)(128)(4,1)}, u32[]{:S(2)}) copy-start(pred[12]{0:T(512)(128)(4,1)} %get-tuple-element.89) | copy-start | bytes 40
  556.2 27.3 %copy-start.16 = (pred[12]{0:T(512)(128)(4,1)S(1)}, pred[12]{0:T(512)(128)(4,1)}, u32[]{:S(2)}) copy-start(pred[12]{0:T(512)(128)(4,1)} %get-tuple-element.94) | copy-start | bytes 40
  567.7 21.1 %copy-start.5 = (bf16[12,8,8,1,128]{4,3,2,1,0:T(2,128)(2,1)S(1)}, bf16[12,8,8,1,128]{4,3,2,1,0:T(2,128)(2,1)}, u32[]{:S(2)}) copy-start(bf16[12,8,8,1,128]{4,3,2,1,0:T(2,128)(2,1)} %get-tuple-element.160) | copy-start | bytes 589828
  574.6 14.2 copy-start.9
  576.8 12.0 copy-start.1
  588.8 8.8 copy-start.4
  588.8 8.8 copy-start.7
  588.8 8.8 copy-start.8
  588.8 8.8 copy-start.10
  588.8 8.8 copy-start.11
  588.8 8.8 copy-start.12
  604.5 731.6 %copy-start.41 = (u32[256]{0:T(256)S(1)}, u32[256]{0:T(256)}, u32[]{:S(2)}) copy-start(u32[256]{0:T(256)} %constant.87) | copy-start | bytes 3076
  604.5 736.3 %copy-start.27 = (pred[12]{0:T(512)(128)(4,1)S(1)}, pred[12]{0:T(512)(128)(4,1)}, u32[]{:S(2)}) copy-start(pred[12]{0:T(512)(128)(4,1)} %copy-done.26) | copy-start | bytes 40
  609.3 19.3 %copy-start.2 = (f32[3456,128]{1,0:T(8,128)S(1)}, f32[3456,128]{1,0:T(8,128)}, u32[]{:S(2)}) copy-start(f32[3456,128]{1,0:T(8,128)} %get-tuple-element.277) | copy-start | bytes 5308420 | tf_op jit(solution)/shard_map/while
  638.8 19.3 %copy-start.2 = (f32[3456,128]{1,0:T(8,128)S(1)}, f32[3456,128]{1,0:T(8,128)}, u32[]{:S(2)}) copy-start(f32[3456,128]{1,0:T(8,128)} %get-tuple-element.277) | copy-start | bytes 5308420 | tf_op jit(solution)/shard_map/while
  668.3 19.3 %copy-start.2 = (f32[3456,128]{1,0:T(8,128)S(1)}, f32[3456,128]{1,0:T(8,128)}, u32[]{:S(2)}) copy-start(f32[3456,128]{1,0:T(8,128)} %get-tuple-element.277) | copy-start | bytes 5308420 | tf_op jit(solution)/shard_map/while
  697.7 19.3 %copy-start.2 = (f32[3456,128]{1,0:T(8,128)S(1)}, f32[3456,128]{1,0:T(8,128)}, u32[]{:S(2)}) copy-start(f32[3456,128]{1,0:T(8,128)} %get-tuple-element.277) | copy-start | bytes 5308420 | tf_op jit(solution)/shard_map/while
  727.2 19.3 %copy-start.2 = (f32[3456,128]{1,0:T(8,128)S(1)}, f32[3456,128]{1,0:T(8,128)}, u32[]{:S(2)}) copy-start(f32[3456,128]{1,0:T(8,128)} %get-tuple-element.277) | copy-start | bytes 5308420 | tf_op jit(solution)/shard_map/while
  756.7 19.3 %copy-start.2 = (f32[3456,128]{1,0:T(8,128)S(1)}, f32[3456,128]{1,0:T(8,128)}, u32[]{:S(2)}) copy-start(f32[3456,128]{1,0:T(8,128)} %get-tuple-element.277) | copy-start | bytes 5308420 | tf_op jit(solution)/shard_map/while
  786.2 19.3 %copy-start.2 = (f32[3456,128]{1,0:T(8,128)S(1)}, f32[3456,128]{1,0:T(8,128)}, u32[]{:S(2)}) copy-start(f32[3456,128]{1,0:T(8,128)} %get-tuple-element.277) | copy-start | bytes 5308420 | tf_op jit(solution)/shard_map/while
  815.7 19.3 %copy-start.2 = (f32[3456,128]{1,0:T(8,128)S(1)}, f32[3456,128]{1,0:T(8,128)}, u32[]{:S(2)}) copy-start(f32[3456,128]{1,0:T(8,128)} %get-tuple-element.277) | copy-start | bytes 5308420 | tf_op jit(solution)/shard_map/while
  845.1 19.3 %copy-start.2 = (f32[3456,128]{1,0:T(8,128)S(1)}, f32[3456,128]{1,0:T(8,128)}, u32[]{:S(2)}) copy-start(f32[3456,128]{1,0:T(8,128)} %get-tuple-element.277) | copy-start | bytes 5308420 | tf_op jit(solution)/shard_map/while
  874.6 19.3 %copy-start.2 = (f32[3456,128]{1,0:T(8,128)S(1)}, f32[3456,128]{1,0:T(8,128)}, u32[]{:S(2)}) copy-start(f32[3456,128]{1,0:T(8,128)} %get-tuple-element.277) | copy-start | bytes 5308420 | tf_op jit(solution)/shard_map/while
  904.1 19.3 %copy-start.2 = (f32[3456,128]{1,0:T(8,128)S(1)}, f32[3456,128]{1,0:T(8,128)}, u32[]{:S(2)}) copy-start(f32[3456,128]{1,0:T(8,128)} %get-tuple-element.277) | copy-start | bytes 5308420 | tf_op jit(solution)/shard_map/while
  933.6 19.3 %copy-start.2 = (f32[3456,128]{1,0:T(8,128)S(1)}, f32[3456,128]{1,0:T(8,128)}, u32[]{:S(2)}) copy-start(f32[3456,128]{1,0:T(8,128)} %get-tuple-element.277) | copy-start | bytes 5308420 | tf_op jit(solution)/shard_map/while
  958.3 382.5 %copy-start.6 = (bf16[12,512,128]{2,1,0:T(8,128)(2,1)S(1)}, bf16[12,512,128]{2,1,0:T(8,128)(2,1)}, u32[]{:S(2)}) copy-start(bf16[12,512,128]{2,1,0:T(8,128)(2,1)} %get-tuple-element.37) | copy-start | bytes 4718596
  1255.1 8.6 collective-permute-start.10
  1256.4 14.2 %collective-permute-start.11 = (f32[32,128]{1,0:T(8,128)S(1)}, f32[32,128]{1,0:T(8,128)S(1)}, u32[]{:S(2)}, u32[]{:S(2)}) collective-permute-start(f32[32,128]{1,0:T(8,128)S(1)} %fusion), channel_id=1, source_target_pairs={{0,16},{2,18},{4,20},{6,22},{8,24},{10,26},{12,28},{14,30},{16,32}... | collective-permute-start | bytes 49160
  1257.7 14.2 %collective-permute-start.12 = (f32[32,128]{1,0:T(8,128)S(1)}, f32[32,128]{1,0:T(8,128)S(1)}, u32[]{:S(2)}, u32[]{:S(2)}) collective-permute-start(f32[32,128]{1,0:T(8,128)S(1)} %fusion), channel_id=1, source_target_pairs={{0,18},{2,20},{4,22},{6,24},{8,26},{10,28},{12,30},{14,32},{16,34}... | collective-permute-start | bytes 49160
  1259.0 14.2 %collective-permute-start.13 = (f32[32,128]{1,0:T(8,128)S(1)}, f32[32,128]{1,0:T(8,128)S(1)}, u32[]{:S(2)}, u32[]{:S(2)}) collective-permute-start(f32[32,128]{1,0:T(8,128)S(1)} %fusion), channel_id=1, source_target_pairs={{0,20},{2,22},{4,24},{6,26},{8,28},{10,30},{12,32},{14,34},{16,36}... | collective-permute-start | bytes 49160
  1260.3 2.1 collective-permute-start.23
  1262.4 16.9 %collective-permute-start.14 = (f32[32,128]{1,0:T(8,128)S(1)}, f32[32,128]{1,0:T(8,128)S(1)}, u32[]{:S(2)}, u32[]{:S(2)}) collective-permute-start(f32[32,128]{1,0:T(8,128)S(1)} %fusion), channel_id=1, source_target_pairs={{0,22},{2,24},{4,26},{6,28},{8,30},{10,32},{12,34},{14,36},{16,38}... | collective-permute-start | bytes 49160
  1263.7 37.7 %collective-permute-start.15 = (f32[32,128]{1,0:T(8,128)S(1)}, f32[32,128]{1,0:T(8,128)S(1)}, u32[]{:S(2)}, u32[]{:S(2)}) collective-permute-start(f32[32,128]{1,0:T(8,128)S(1)} %fusion), channel_id=1, source_target_pairs={{0,24},{2,26},{4,28},{6,30},{8,32},{10,34},{12,36},{14,38},{16,40}... | collective-permute-start | bytes 49160
  1270.6 33.4 %collective-permute-start.16 = (f32[32,128]{1,0:T(8,128)S(1)}, f32[32,128]{1,0:T(8,128)S(1)}, u32[]{:S(2)}, u32[]{:S(2)}) collective-permute-start(f32[32,128]{1,0:T(8,128)S(1)} %fusion), channel_id=1, source_target_pairs={{0,26},{2,28},{4,30},{6,32},{8,34},{10,36},{12,38},{14,40},{16,42}... | collective-permute-start | bytes 49160
  1271.9 40.0 %collective-permute-start.17 = (f32[32,128]{1,0:T(8,128)S(1)}, f32[32,128]{1,0:T(8,128)S(1)}, u32[]{:S(2)}, u32[]{:S(2)}) collective-permute-start(f32[32,128]{1,0:T(8,128)S(1)} %fusion), channel_id=1, source_target_pairs={{0,28},{2,30},{4,32},{6,34},{8,36},{10,38},{12,40},{14,42},{16,44}... | collective-permute-start | bytes 49160
  1273.2 43.6 %collective-permute-start.18 = (f32[32,128]{1,0:T(8,128)S(1)}, f32[32,128]{1,0:T(8,128)S(1)}, u32[]{:S(2)}, u32[]{:S(2)}) collective-permute-start(f32[32,128]{1,0:T(8,128)S(1)} %fusion), channel_id=1, source_target_pairs={{0,30},{2,32},{4,34},{6,36},{8,38},{10,40},{12,42},{14,44},{16,46}... | collective-permute-start | bytes 49160
  1279.3 39.7 %collective-permute-start.19 = (f32[32,128]{1,0:T(8,128)S(1)}, f32[32,128]{1,0:T(8,128)S(1)}, u32[]{:S(2)}, u32[]{:S(2)}) collective-permute-start(f32[32,128]{1,0:T(8,128)S(1)} %fusion), channel_id=1, source_target_pairs={{0,32},{2,34},{4,36},{6,38},{8,40},{10,42},{12,44},{14,46},{16,48}... | collective-permute-start | bytes 49160
  1301.4 19.5 %collective-permute-start.20 = (f32[32,128]{1,0:T(8,128)S(1)}, f32[32,128]{1,0:T(8,128)S(1)}, u32[]{:S(2)}, u32[]{:S(2)}) collective-permute-start(f32[32,128]{1,0:T(8,128)S(1)} %fusion), channel_id=1, source_target_pairs={{0,34},{2,36},{4,38},{6,40},{8,42},{10,44},{12,46},{14,48},{16,50}... | collective-permute-start | bytes 49160
  1304.0 21.5 %collective-permute-start.21 = (f32[32,128]{1,0:T(8,128)S(1)}, f32[32,128]{1,0:T(8,128)S(1)}, u32[]{:S(2)}, u32[]{:S(2)}) collective-permute-start(f32[32,128]{1,0:T(8,128)S(1)} %fusion), channel_id=1, source_target_pairs={{0,36},{2,38},{4,40},{6,42},{8,44},{10,46},{12,48},{14,50},{16,52}... | collective-permute-start | bytes 49160
  1311.9 18.0 %collective-permute-start.22 = (f32[32,128]{1,0:T(8,128)S(1)}, f32[32,128]{1,0:T(8,128)S(1)}, u32[]{:S(2)}, u32[]{:S(2)}) collective-permute-start(f32[32,128]{1,0:T(8,128)S(1)} %fusion), channel_id=1, source_target_pairs={{0,38},{2,40},{4,42},{6,44},{8,46},{10,48},{12,50},{14,52},{16,54}... | collective-permute-start | bytes 49160
  1316.8 17.1 %collective-permute-start.4 = (f32[32,128]{1,0:T(8,128)S(1)}, f32[32,128]{1,0:T(8,128)S(1)}, u32[]{:S(2)}, u32[]{:S(2)}) collective-permute-start(f32[32,128]{1,0:T(8,128)S(1)} %fusion), channel_id=1, source_target_pairs={{0,2},{2,4},{4,6},{6,8},{8,10},{10,12},{12,14},{14,16},{16,18},{18... | collective-permute-start | bytes 49160
  1319.0 18.4 %collective-permute-start.5 = (f32[32,128]{1,0:T(8,128)S(1)}, f32[32,128]{1,0:T(8,128)S(1)}, u32[]{:S(2)}, u32[]{:S(2)}) collective-permute-start(f32[32,128]{1,0:T(8,128)S(1)} %fusion), channel_id=1, source_target_pairs={{0,4},{2,6},{4,8},{6,10},{8,12},{10,14},{12,16},{14,18},{16,20},{1... | collective-permute-start | bytes 49160
  1321.0 16.4 %collective-permute-start.6 = (f32[32,128]{1,0:T(8,128)S(1)}, f32[32,128]{1,0:T(8,128)S(1)}, u32[]{:S(2)}, u32[]{:S(2)}) collective-permute-start(f32[32,128]{1,0:T(8,128)S(1)} %fusion), channel_id=1, source_target_pairs={{0,6},{2,8},{4,10},{6,12},{8,14},{10,16},{12,18},{14,20},{16,22},{... | collective-permute-start | bytes 49160
  1325.5 11.9 collective-permute-start.7
  1329.9 7.5 collective-permute-start.8
  1333.9 3.5 collective-permute-start.9
  (26 other events, 104.4 us)
Sparse Core Ops, SparseCore 0:
  1340.9 70.6 reduce-scatter.5
